TPU v7x, 256 devices: a whole 4x4x8 slice. The times are simulated.
256 devices in a mesh: section: 16 (over y_hi, z), seq: 16 (over y_lo, x, core).
Axes of the slice: x: 4, y: 4 (y_hi: 2, y_lo: 2; y = y_hi * 2 + y_lo), z: 8, core: 2. Of those that a mesh axis runs over, the one named last changes fastest.
Arguments:
- stream: bfloat16 [16, 2048, 2048], P('section', 'seq'), may hold values from -6 to 6
- queries: bfloat16 [16, 2048, 2048], P('section', 'seq'), may hold values from -5 to 5
- key_rows: bfloat16 [16, 2048, 2048], P('section', 'seq'), may hold values from -5 to 5
- value_rows: bfloat16 [16, 2048, 2048], P('section', 'seq'), may hold values from -6 to 6
- o_weight: bfloat16 [16, 2048, 2048], P('section', 'seq'), may hold values from -0.125 to 0.125
- norm_gain: float32 [16, 2048], P('section'), may hold values from 0.1 to 1.9
- w_gate: bfloat16 [16, 2048, 7168], P('section', None, 'seq'), may hold values from -0.125 to 0.125
- w_up: bfloat16 [16, 2048, 7168], P('section', None, 'seq'), may hold values from -0.125 to 0.125
- w_down: bfloat16 [16, 7168, 2048], P('section', 'seq'), may hold values from -0.0625 to 0.0625
Outputs:
- passed: bfloat16 [16, 2048, 2048], P('section', 'seq')
All inputs are finite; a program needn't handle non-finite values.
Results may differ from a plain program's by a relative error of at most 0.012.
Values may be sent and summed in bfloat16 or wider, within the bound.
No kernel may reach another device: no remote copies, remote signals or barrier semaphores. Data moves between devices by JAX's collectives and lax.ppermute only.
A program may use at most 64 MiB of HBM per device.

v0:
```python
import jax
import jax.numpy as jnp
import numpy as np
from jax import lax
from jax.experimental import pallas as pl
from jax.experimental.pallas import tpu as pltpu
from jax.sharding import Mesh, PartitionSpec as P

HEAD_DIM = 128
T = 128
D = 2048
SEQ = ("y", "x", "c")
BF = jnp.bfloat16
F32 = jnp.float32
VMEM = pl.BlockSpec(memory_space=pltpu.VMEM)
MB = 1 << 20
HBM = pl.BlockSpec(memory_space=pltpu.MemorySpace.HBM)
ANY = pl.BlockSpec(memory_space=pl.ANY)
SMEM = pl.BlockSpec(memory_space=pltpu.SMEM)


def chip_shift(v, dy, dx):
    route = []
    for y in range(2):
        for x in range(4):
            route.append((y * 4 + x, ((y + dy) % 2) * 4 + (x + dx) % 4))
    return lax.ppermute(v, ("y", "x"), route)


def to_plus(v):
    return chip_shift(v, 0, 1)


def to_minus(v):
    return chip_shift(v, 0, -1)


def to_side(v):
    return chip_shift(v, 1, 0)


def to_core(v):
    return lax.ppermute(v, "c", [(0, 1), (1, 0)])


THIRDS = (0, 48, 96, 128)


FIRST = ((0, 0), (0, -1), (0, 1), (1, 0))
SECOND = ((1, -1), (0, 2), (1, 1))


def gather_first(own):
    return {(0, 0): own, (0, -1): to_plus(own), (0, 1): to_minus(own), (1, 0): to_side(own)}


def gather_second(first):
    p, s = first[0, 1], first[1, 0]
    return {(1, -1): to_plus(s), (0, 2): to_minus(p), (1, 1): to_side(p)}


def gather_third(second):
    a, b, c, d = THIRDS
    return (to_side(second[0, 2][a:b]), to_minus(second[1, 1][b:c]), to_plus(second[1, -1][c:d]))


def pack_kernel(q, k, v, out, held, sem):
    copies = [pltpu.make_async_copy(ref, held.at[n], sem.at[n]) for n, ref in enumerate((q, k, v))]
    for copy in copies:
        copy.start()
    for n, copy in enumerate(copies):
        copy.wait()
        for j in range(16):
            out[j, :, n * 128 : (n + 1) * 128] = held[n, :, j * HEAD_DIM : (j + 1) * HEAD_DIM]


def pack(q, k, v):
    return pl.pallas_call(
        pack_kernel,
        out_shape=jax.ShapeDtypeStruct((16, T, 384), BF),
        in_specs=[HBM] * 3,
        out_specs=VMEM,
        scratch_shapes=[pltpu.VMEM((3, T, D), BF), pltpu.SemaphoreType.DMA((3,))],
        name="pack",
    )(q, k, v)


QB = 256
SPAN = 1024


def attend_kernel(qkv, out):
    scale = HEAD_DIM ** -0.5
    row = lax.broadcasted_iota(jnp.int32, (QB, SPAN), 0)
    col = lax.broadcasted_iota(jnp.int32, (QB, SPAN), 1)
    dims = (((1,), (1,)), ((), ()))
    for lo in range(0, 2048, SPAN):
        hi = lo + SPAN

        def block(j, carry, lo=lo, hi=hi):
            rows = pl.ds(lo + j * QB, QB)
            q = qkv[rows, 0:128]
            sd = lax.dot_general(q, qkv[lo:hi, 128:256], dims, preferred_element_type=F32) * scale
            sd = jnp.where(col <= row + j * QB, sd, -1e30)
            top = jnp.max(sd, axis=-1, keepdims=True)
            if lo > 0:
                sl = lax.dot_general(q, qkv[0:lo, 128:256], dims, preferred_element_type=F32) * scale
                top = jnp.maximum(top, jnp.max(sl, axis=-1, keepdims=True))
            ed = jnp.exp(sd - top)
            total = jnp.sum(ed, axis=-1, keepdims=True)
            mix = jnp.dot(ed.astype(BF), qkv[lo:hi, 256:384], preferred_element_type=F32)
            if lo > 0:
                el = jnp.exp(sl - top)
                total = total + jnp.sum(el, axis=-1, keepdims=True)
                mix = mix + jnp.dot(el.astype(BF), qkv[0:lo, 256:384], preferred_element_type=F32)
            out[rows, :] = (mix / total).astype(BF)
            return carry

        lax.fori_loop(0, SPAN // QB, block, 0)


def attend(qkv):
    return pl.pallas_call(
        attend_kernel,
        out_shape=jax.ShapeDtypeStruct((2048, HEAD_DIM), BF),
        in_specs=[VMEM],
        out_specs=VMEM,
        cost_estimate=pl.CostEstimate(flops=1_200_000_000, bytes_accessed=2_097_152, transcendentals=2_400_000),
        compiler_params=pltpu.CompilerParams(vmem_limit_bytes=28 * MB),
        name="attend",
    )(qkv)


CHUNK = 512


def project_kernel(place, att, *refs):
    weights, (mine, theirs, left, held, acc, sem) = refs[:-6], refs[-6:]
    copies, row = [], 0
    for w in weights:
        copies.append((row, pltpu.make_async_copy(w, held.at[pl.ds(row, w.shape[0]), :], sem.at[len(copies)])))
        row += w.shape[0]
    for _, copy in copies:
        copy.start()
    core = place[8]
    for k in range(8):
        left[0:T, k * 128 : (k + 1) * 128] = att[place[k], pl.ds(core * T, T), :]
        left[T : 2 * T, k * 128 : (k + 1) * 128] = att[place[k], pl.ds((1 - core) * T, T), :]
    for lo in range(0, 1024, CHUNK):
        for at, copy in copies:
            if lo <= at < lo + CHUNK:
                copy.wait()

        def columns(n, carry, lo=lo):
            cols = pl.ds(n * CHUNK, CHUNK)
            part = jnp.dot(left[:, lo : lo + CHUNK], held[lo : lo + CHUNK, cols], preferred_element_type=F32)
            if lo == 0:
                acc[:, cols] = part
            else:
                acc[:, cols] += part
            return carry

        lax.fori_loop(0, D // CHUNK, columns, 0)
    mine[...] = acc[0:T, :]
    theirs[...] = acc[T : 2 * T, :].astype(BF)


def project(place, att, weights):
    return pl.pallas_call(
        project_kernel,
        out_shape=(jax.ShapeDtypeStruct((T, D), F32), jax.ShapeDtypeStruct((T, D), BF)),
        in_specs=[SMEM, VMEM] + [ANY] * len(weights),
        out_specs=(VMEM,) * 2,
        scratch_shapes=[
            pltpu.VMEM((2 * T, 1024), BF),
            pltpu.VMEM((1024, D), BF),
            pltpu.VMEM((2 * T, D), F32),
            pltpu.SemaphoreType.DMA((len(weights),)),
        ],
        cost_estimate=pl.CostEstimate(flops=1_100_000_000, bytes_accessed=6_000_000, transcendentals=0),
        compiler_params=pltpu.CompilerParams(vmem_limit_bytes=20 * MB),
        name="project",
    )(place, att, *weights)


def norm_kernel(mine, other, stream, gain, resid, normed):
    acc = stream[...].astype(F32) + mine[...] + other[...].astype(F32)
    resid[...] = acc
    mean = jnp.mean(acc * acc, axis=-1, keepdims=True)
    normed[...] = (acc * lax.rsqrt(mean + 1e-5) * gain[...]).astype(BF)


def norm(mine, other, stream, gain):
    return pl.pallas_call(
        norm_kernel,
        out_shape=(jax.ShapeDtypeStruct((T, D), F32), jax.ShapeDtypeStruct((T, D), BF)),
        in_specs=[VMEM] * 4,
        out_specs=(VMEM,) * 2,
        compiler_params=pltpu.CompilerParams(vmem_limit_bytes=8 * MB),
        name="norm",
    )(mine, other, stream, gain)


def stack_kernel(axis, *refs):
    parts, out, sem = refs[:-2], refs[-2], refs[-1]
    copies = []
    for n, part in enumerate(parts):
        place = out.at[n] if axis == 0 else out.at[:, n]
        copies.append(pltpu.make_async_copy(part, place, sem.at[n]))
    for copy in copies:
        copy.start()
    for copy in copies:
        copy.wait()


def stack(parts, axis, space):
    n = len(parts)
    shape = parts[0].shape[:axis] + (n,) + parts[0].shape[axis:]
    return pl.pallas_call(
        lambda *refs: stack_kernel(axis, *refs),
        out_shape=jax.ShapeDtypeStruct(shape, BF),
        in_specs=[ANY] * n,
        out_specs=space,
        scratch_shapes=[pltpu.SemaphoreType.DMA((n,))],
        compiler_params=pltpu.CompilerParams(vmem_limit_bytes=14 * MB),
        name="stack",
    )(*parts)


NT = (((1,), (1,)), ((), ()))


def ffn_kernel(count, *refs):
    shards, weights, outs = refs[:count], refs[count], refs[count + 1 : -2]
    x, acc = refs[-2:]
    row = 0
    for v in shards:
        x[row : row + v.shape[0], :] = v[...]
        row += v.shape[0]

    block = min(x.shape[0], 128) if x.shape[0] == 512 else x.shape[0]

    def step(i, carry):
        part = i % 2
        rows = pl.ds((i // 2) * block, block)
        gate = lax.dot_general(x[rows, :], weights[0, part], NT, preferred_element_type=F32)
        gate = gate / (1.0 + jnp.exp(-gate))
        up = lax.dot_general(x[rows, :], weights[1, part], NT, preferred_element_type=F32)
        hidden = (gate * up).astype(BF)
        share = jnp.dot(hidden, weights[2, part], preferred_element_type=F32)
        acc[rows, :] = jnp.where(part == 0, 0.0, acc[rows, :]) + share
        return carry

    lax.fori_loop(0, 2 * (x.shape[0] // block), step, 0)
    row = 0
    for o in outs:
        o[...] = acc[row : row + o.shape[0], :].astype(BF)
        row += o.shape[0]


def ffn(shards, weights, sizes=None):
    n = len(shards)
    sizes = sizes or [v.shape[0] for v in shards]
    tokens = sum(sizes)
    return pl.pallas_call(
        lambda *refs: ffn_kernel(n, *refs),
        out_shape=tuple(jax.ShapeDtypeStruct((size, D), BF) for size in sizes),
        in_specs=[VMEM] * (n + 1),
        out_specs=(VMEM,) * len(sizes),
        scratch_shapes=[pltpu.VMEM((tokens, D), BF), pltpu.VMEM((tokens, D), F32)],
        cost_estimate=pl.CostEstimate(
            flops=6 * tokens * 2048 * 896, bytes_accessed=tokens * 8192, transcendentals=tokens * 896
        ),
        compiler_params=pltpu.CompilerParams(vmem_limit_bytes=24 * MB),
        name="ffn",
    )(*shards, weights)


SPLIT = 2
H = T // SPLIT


def merge_kernel(*refs):
    pieces, returned, outs = refs[0:3], refs[3:6], refs[6:]
    for n in range(3):
        lo, hi = THIRDS[n], THIRDS[n + 1]
        for h in range(SPLIT):
            out, start = outs[SPLIT * n + h], h * H
            out[...] = pieces[n][start : start + H, :]
            a, b = max(lo, start), min(hi, start + H)
            if a < b:
                both = pieces[n][a:b, :].astype(F32) + returned[n][a - lo : b - lo, :].astype(F32)
                out[a - start : b - start, :] = both.astype(BF)


def merge(pieces, returned):
    return pl.pallas_call(
        merge_kernel,
        out_shape=(jax.ShapeDtypeStruct((H, D), BF),) * (3 * SPLIT),
        in_specs=[VMEM] * 6,
        out_specs=(VMEM,) * (3 * SPLIT),
        compiler_params=pltpu.CompilerParams(vmem_limit_bytes=10 * MB),
        name="merge",
    )(*pieces, *returned)


def finish_kernel(start, residual, own, v0, v1, v2, out):
    total = residual[start : start + H, :] + own[...].astype(F32)
    for v in (v0, v1, v2):
        total = total + v[...].astype(F32)
    out[...] = total.astype(BF)


def finish(start, *vs):
    return pl.pallas_call(
        lambda *refs: finish_kernel(start, *refs),
        out_shape=jax.ShapeDtypeStruct((H, D), BF),
        in_specs=[VMEM] * 5,
        out_specs=VMEM,
        compiler_params=pltpu.CompilerParams(vmem_limit_bytes=6 * MB),
        name="finish",
    )(*vs)


def added(*vs):
    acc = vs[0].astype(F32)
    for v in vs[1:]:
        acc = acc + v.astype(F32)
    return acc.astype(BF)


def layer(stream, queries, key_rows, value_rows, o_weight, norm_gain, w_gate, w_up, w_down):
    y, x, c = (lax.axis_index(n) for n in SEQ)
    first = gather_first(o_weight[0])
    packed = pack(queries[0], key_rows[0], value_rows[0])
    qkv = lax.all_to_all(packed, SEQ, split_axis=0, concat_axis=0, tiled=True)
    own = stack((w_gate[0].T, w_up[0].T, w_down[0]), 0, ANY)
    across = to_core(own)
    weights = stack((own, across), 1, VMEM)
    second = gather_second(first)
    attended = attend(qkv.reshape(2048, 384))
    blocks = attended.reshape(8, 2 * T, HEAD_DIM)
    returned = lax.all_to_all(blocks, ("y", "x"), split_axis=0, concat_axis=0, tiled=True)
    pieces = [first[k] for k in FIRST] + [second[k] for k in SECOND]
    pieces += list(gather_third(second))
    order = [((y + dy) % 2) * 4 + (x + dx) % 4 for dy, dx in FIRST + SECOND + ((1, 2),)]
    place = jnp.stack(order + [c]).astype(jnp.int32)
    mine, theirs = project(place, returned, pieces)
    residual, normed = norm(mine, to_core(theirs), stream[0], norm_gain)

    first = gather_first(normed)
    second = gather_second(first)
    outs = ffn([first[k] for k in FIRST], weights, [H] * (4 * SPLIT))
    outs, second = lax.optimization_barrier((outs, second))
    far = ffn(list(gather_third(second)), weights)
    far, second = lax.optimization_barrier((far, [second[k] for k in SECOND]))
    r0 = to_side(far[0])
    r1 = to_plus(far[1])
    r2 = to_minus(far[2])
    sm_, pp_, sp_ = ffn(second, weights)
    merged = merge((pp_, sp_, sm_), (r0, r1, r2))
    shares = []
    for h in range(SPLIT):
        pp_, sp_, sm_ = merged[h::SPLIT]
        shares.append((to_minus(sm_), to_plus(pp_), to_side(sp_)))
    done = []
    for h in range(SPLIT):
        t0, t1, t2 = shares[h]
        own_, m_, p_, s_ = outs[h::SPLIT]
        s_ = added(s_, t0)
        p_ = added(p_, t1, t2)
        arrived = to_minus(m_), to_plus(p_), to_side(s_)
        total = finish(h * H, residual, own_, *arrived)
        done.append(lax.ppermute(total, "s", [((i - 1) % 16, i) for i in range(16)]))
    return jnp.concatenate(done, 0)[None]


def solution(mesh):
    fine = Mesh(np.asarray(mesh.devices).reshape(16, 2, 4, 2), ("s", "y", "x", "c"))
    rows = P("s", SEQ, None)
    placed = (rows, rows, rows, rows, rows, P("s", None), P("s", None, SEQ), P("s", None, SEQ), rows)
    return jax.shard_map(layer, mesh=fine, in_specs=placed, out_specs=rows, check_vma=False)
```

profile of v0, /device:TPU:4, one launch (start us, length us, event | category | flops | bytes accessed | tf_op | source)
XLA Modules:
  0.0 197.8 jit_solution(1233165501613825095)
XLA Ops:
  0.0 1.5 copy-done
  1.5 1.5 copy-done.1
  4.5 2.5 %stack.42.refs_0_ = bf16[3,448,2048]{2,1,0:T(8,128)(2,1)} custom-call(bf16[448,2048]{1,0:T(8,128)(2,1)S(1)} %bitcast.25, bf16[448,2048]{1,0:T(8,128)(2,1)S(1)} %bitcast.26, bf16[448,2048]{1,0:T(8,128)(2,1)S(1)} %bitcast.27), custom_call_target="tpu_custom_call" | custom-call | tf_op jit(solution)/shard_map/stack/pallas_call | solution.py:219
  7.1 2.7 %pack.1 = bf16[16,128,384]{2,1,0:T(8,128)(2,1)} custom-call(bf16[128,2048]{1,0:T(8,128)(2,1)} %bitcast.35, bf16[128,2048]{1,0:T(8,128)(2,1)} %bitcast.36, bf16[128,2048]{1,0:T(8,128)(2,1)} %bitcast.37), custom_call_target="tpu_custom_call" | custom-call | tf_op jit(solution)/shard_map/pack/pallas_call | solution.py:78
  9.8 6.1 %all-to-all-start = ((bf16[16,128,384]{2,1,0:T(8,128)(2,1)}), bf16[16,128,384]{2,1,0:T(8,128)(2,1)S(1)}, u32[]{:S(2)}, u32[]{:S(2)}) async-start(bf16[16,128,384]{2,1,0:T(8,128)(2,1)} %pack.1), calls=%async_computation | async-start | bytes 3145728 | tf_op jit(solution)/shard_map/all_to_all | solution.py:336
  18.0 29.2 %collective-permute-done.1.refs_2_ = bf16[128,2048]{1,0:T(8,128)(2,1)} collective-permute-done((bf16[128,2048]{1,0:T(8,128)(2,1)S(1)}, bf16[128,2048]{1,0:T(8,128)(2,1)}, u32[]{:S(2)}, u32[]{:S(2)}) %collective-permute-start.1) | collective-permute-done | bytes 524320 | tf_op jit(solution)/shard_map/ppermute | solution.py:27
  52.0 7.5 %attend.1 = bf16[2048,128]{1,0:T(8,128)(2,1)S(1)} custom-call(bf16[2048,384]{1,0:T(8,128)(2,1)S(1)} %bitcast.28), custom_call_target="tpu_custom_call" | custom-call | flops 1200000000 | bytes 2097152 | tf_op jit(solution)/shard_map/attend/pallas_call | solution.py:123
  60.3 5.1 %all-to-all-start.1 = ((bf16[8,256,128]{2,1,0:T(8,128)(2,1)}), bf16[8,256,128]{2,1,0:T(8,128)(2,1)S(1)}, u32[]{:S(2)}, u32[]{:S(2)}) async-start(bf16[8,256,128]{2,1,0:T(8,128)(2,1)} %bitcast.33), calls=%async_computation.1 | async-start | bytes 1048576 | tf_op jit(solution)/shard_map/all_to_all | solution.py:343
  71.1 6.4 %collective-permute-done.refs_1_ = bf16[128,2048]{1,0:T(8,128)(2,1)} collective-permute-done((bf16[128,2048]{1,0:T(8,128)(2,1)}, bf16[128,2048]{1,0:T(8,128)(2,1)}, u32[]{:S(2)}, u32[]{:S(2)}) %collective-permute-start) | collective-permute-done | bytes 524320 | tf_op jit(solution)/shard_map/ppermute | solution.py:27
  77.5 4.4 %collective-permute-done.8.refs_9_ = bf16[32,2048]{1,0:T(8,128)(2,1)} collective-permute-done((bf16[32,2048]{1,0:T(8,128)(2,1)}, bf16[32,2048]{1,0:T(8,128)(2,1)}, u32[]{:S(2)}, u32[]{:S(2)}) %collective-permute-start.8) | collective-permute-done | bytes 131104 | tf_op jit(solution)/shard_map/ppermute | solution.py:27
  81.9 4.6 %project.1 = (f32[128,2048]{1,0:T(8,128)S(1)}, bf16[128,2048]{1,0:T(8,128)(2,1)S(1)}) custom-call(s32[9]{0:T(128)S(1)} %stack.41.place, bf16[8,256,128]{2,1,0:T(8,128)(2,1)S(1)} %all-to-all-done.1.att, bf16[128,2048]{1,0:T(8,128)(2,1)S(1)} %bitcast.32, bf16[128,2048]{1,0:T(8,128)(2,1)} %collective-permute-done.refs_1_, ...), custom_call_target="tpu_custom_call" | custom-call | flops 1100000000 | bytes 6000000 | tf_op jit(solution)/shard_map/project/pallas_call | solution.py:169
  86.6 1.9 collective-permute-done.9.other
  91.6 11.3 %collective-permute-done.11.refs_2_ = bf16[128,2048]{1,0:T(8,128)(2,1)S(1)} collective-permute-done((bf16[128,2048]{1,0:T(8,128)(2,1)S(1)}, bf16[128,2048]{1,0:T(8,128)(2,1)S(1)}, u32[]{:S(2)}, u32[]{:S(2)}) %collective-permute-start.11) | collective-permute-done | bytes 524320 | tf_op jit(solution)/shard_map/ppermute | solution.py:27
  106.5 4.2 %stack.43.refs_4_.refs_3_ = bf16[3,2,448,2048]{3,2,1,0:T(8,128)(2,1)S(1)} custom-call(bf16[3,448,2048]{2,1,0:T(8,128)(2,1)} %stack.42.refs_0_, bf16[3,448,2048]{2,1,0:T(8,128)(2,1)} %collective-permute-done.13.refs_1_), custom_call_target="tpu_custom_call" | custom-call | tf_op jit(solution)/shard_map/stack/pallas_call | solution.py:219
  110.8 13.0 %ffn.3 = (bf16[64,2048]{1,0:T(8,128)(2,1)S(1)}, bf16[64,2048]{1,0:T(8,128)(2,1)S(1)}, bf16[64,2048]{1,0:T(8,128)(2,1)S(1)}, bf16[64,2048]{1,0:T(8,128)(2,1)S(1)}...) custom-call(bf16[128,2048]{1,0:T(8,128)(2,1)S(1)} %get-tuple-element, ...), custom_call_target="tpu_custom_call" | custom-call | flops 5637144576 | bytes 4194304 | tf_op jit(solution)/shard_map/ffn/pallas_call | solution.py:265
  126.1 2.4 %collective-permute-start.20 = (bf16[32,2048]{1,0:T(8,128)(2,1)S(1)}, bf16[32,2048]{1,0:T(8,128)(2,1)S(1)}, u32[]{:S(2)}, u32[]{:S(2)}) collective-permute-start(bf16[32,2048]{1,0:T(8,128)(2,1)S(1)} %slice.23), channel_id=1, source_target_pairs={{0,2},{2,4},{4,6},{6,0},{8,10},{10,12},{12,14},{14,8},{1,3},{3,5},... | collective-permute-start | bytes 393224 | tf_op jit(solution)/shard_map/ppermute | solution.py:27
  128.5 2.6 %collective-permute-done.20.refs_2_ = bf16[32,2048]{1,0:T(8,128)(2,1)S(1)} collective-permute-done((bf16[32,2048]{1,0:T(8,128)(2,1)S(1)}, bf16[32,2048]{1,0:T(8,128)(2,1)S(1)}, u32[]{:S(2)}, u32[]{:S(2)}) %collective-permute-start.20) | collective-permute-done | bytes 131104 | tf_op jit(solution)/shard_map/ppermute | solution.py:27
  132.1 3.2 %ffn.4 = (bf16[48,2048]{1,0:T(8,128)(2,1)S(1)}, bf16[48,2048]{1,0:T(8,128)(2,1)S(1)}, bf16[32,2048]{1,0:T(8,128)(2,1)S(1)}) custom-call(bf16[48,2048]{1,0:T(8,128)(2,1)S(1)} %collective-permute-done.18.refs_0_, bf16[48,2048]{1,0:T(8,128)(2,1)S(1)} %collective-permute-done.19.refs_1_, bf16[32,2048]{1,0:T(8,128)(2,1)S(1)} %collective-permute-done.20.refs_2_, ...), custom_call_target="tpu_custom_call" | custom-call | flops 1409286144 | bytes 1048576 | tf_op jit(solution)/shard_map/ffn/pallas_call | solution.py:265
  136.3 3.2 %collective-permute-start.22 = (bf16[48,2048]{1,0:T(8,128)(2,1)S(1)}, bf16[48,2048]{1,0:T(8,128)(2,1)S(1)}, u32[]{:S(2)}, u32[]{:S(2)}) collective-permute-start(bf16[48,2048]{1,0:T(8,128)(2,1)S(1)} %get-tuple-element.74), channel_id=1, source_target_pairs={{0,2},{2,4},{4,6},{6,0},{8,10},{10,12},{12,14},{14,8},{1,3},{3,5},... | collective-permute-start | bytes 589832 | tf_op jit(solution)/shard_map/ppermute | solution.py:27
  139.5 5.5 %ffn.5 = (bf16[128,2048]{1,0:T(8,128)(2,1)S(1)}, bf16[128,2048]{1,0:T(8,128)(2,1)S(1)}, bf16[128,2048]{1,0:T(8,128)(2,1)S(1)}) custom-call(bf16[128,2048]{1,0:T(8,128)(2,1)S(1)} %collective-permute-done.15.refs_0_, bf16[128,2048]{1,0:T(8,128)(2,1)S(1)} %collective-permute-done.14.refs_1_, bf16[128,2048]{1,0:T(8,128)(2,1)S(1)} %collective-permute-done.16.refs_2_, ...), custom_call_target="tpu_custom_call" | custom-call | flops 4227858432 | bytes 3145728 | tf_op jit(solution)/shard_map/ffn/pallas_call | solution.py:265
  146.5 3.2 %collective-permute-start.31 = (bf16[64,2048]{1,0:T(8,128)(2,1)S(1)}, bf16[64,2048]{1,0:T(8,128)(2,1)S(1)}, u32[]{:S(2)}, u32[]{:S(2)}) collective-permute-start(bf16[64,2048]{1,0:T(8,128)(2,1)S(1)} %get-tuple-element.83), channel_id=1, source_target_pairs={{0,2},{2,4},{4,6},{6,0},{8,10},{10,12},{12,14},{14,8},{1,3},{3,5},... | collective-permute-start | bytes 786440 | tf_op jit(solution)/shard_map/ppermute | solution.py:27
  149.7 2.0 %collective-permute-start.17 = (bf16[64,2048]{1,0:T(8,128)(2,1)S(1)}, bf16[64,2048]{1,0:T(8,128)(2,1)S(1)}, u32[]{:S(2)}, u32[]{:S(2)}) collective-permute-start(bf16[64,2048]{1,0:T(8,128)(2,1)S(1)} %get-tuple-element.59), channel_id=1, source_target_pairs={{0,6},{2,0},{4,2},{6,4},{8,14},{10,8},{12,10},{14,12},{1,7},{3,1},... | collective-permute-start | bytes 786440 | tf_op jit(solution)/shard_map/ppermute | solution.py:27
  151.8 3.2 %collective-permute-start.34 = (bf16[64,2048]{1,0:T(8,128)(2,1)S(1)}, bf16[64,2048]{1,0:T(8,128)(2,1)S(1)}, u32[]{:S(2)}, u32[]{:S(2)}) collective-permute-start(bf16[64,2048]{1,0:T(8,128)(2,1)S(1)} %get-tuple-element.86), channel_id=1, source_target_pairs={{0,6},{2,0},{4,2},{6,4},{8,14},{10,8},{12,10},{14,12},{1,7},{3,1},... | collective-permute-start | bytes 786440 | tf_op jit(solution)/shard_map/ppermute | solution.py:27
  156.1 2.6 %collective-permute-start.24 = (bf16[64,2048]{1,0:T(8,128)(2,1)S(1)}, bf16[64,2048]{1,0:T(8,128)(2,1)S(1)}, u32[]{:S(2)}, u32[]{:S(2)}) collective-permute-start(bf16[64,2048]{1,0:T(8,128)(2,1)S(1)} %get-tuple-element.76), channel_id=1, source_target_pairs={{0,2},{2,4},{4,6},{6,0},{8,10},{10,12},{12,14},{14,8},{1,3},{3,5},... | collective-permute-start | bytes 786440 | tf_op jit(solution)/shard_map/ppermute | solution.py:27
  158.8 8.3 %collective-permute-done.34 = bf16[64,2048]{1,0:T(8,128)(2,1)S(1)} collective-permute-done((bf16[64,2048]{1,0:T(8,128)(2,1)S(1)}, bf16[64,2048]{1,0:T(8,128)(2,1)S(1)}, u32[]{:S(2)}, u32[]{:S(2)}) %collective-permute-start.34) | collective-permute-done | bytes 262176 | tf_op jit(solution)/shard_map/ppermute | solution.py:27
  167.2 3.0 %collective-permute-start.33 = (bf16[64,2048]{1,0:T(8,128)(2,1)S(1)}, bf16[64,2048]{1,0:T(8,128)(2,1)S(1)}, u32[]{:S(2)}, u32[]{:S(2)}) collective-permute-start(bf16[64,2048]{1,0:T(8,128)(2,1)S(1)} %add_convert_fusion.1), channel_id=1, source_target_pairs={{0,2},{2,4},{4,6},{6,0},{8,10},{10,12},{12,14},{14,8},{1,3},{3,5},... | collective-permute-start | bytes 786440 | tf_op jit(solution)/shard_map/ppermute | solution.py:27
  171.2 3.2 %collective-permute-done.27 = bf16[64,2048]{1,0:T(8,128)(2,1)S(1)} collective-permute-done((bf16[64,2048]{1,0:T(8,128)(2,1)S(1)}, bf16[64,2048]{1,0:T(8,128)(2,1)S(1)}, u32[]{:S(2)}, u32[]{:S(2)}) %collective-permute-start.27) | collective-permute-done | bytes 262176 | tf_op jit(solution)/shard_map/ppermute | solution.py:27
  174.4 3.2 %collective-permute-start.26 = (bf16[64,2048]{1,0:T(8,128)(2,1)S(1)}, bf16[64,2048]{1,0:T(8,128)(2,1)S(1)}, u32[]{:S(2)}, u32[]{:S(2)}) collective-permute-start(bf16[64,2048]{1,0:T(8,128)(2,1)S(1)} %add_convert_fusion.3), channel_id=1, source_target_pairs={{0,2},{2,4},{4,6},{6,0},{8,10},{10,12},{12,14},{14,8},{1,3},{3,5},... | collective-permute-start | bytes 786440 | tf_op jit(solution)/shard_map/ppermute | solution.py:27
  179.3 2.0 %collective-permute-start.36 = (bf16[64,2048]{1,0:T(8,128)(2,1)S(1)}, bf16[64,2048]{1,0:T(8,128)(2,1)S(1)}, u32[]{:S(2)}, u32[]{:S(2)}) collective-permute-start(bf16[64,2048]{1,0:T(8,128)(2,1)S(1)} %finish.3), channel_id=1, source_target_pairs={{240,0},{0,16},{16,32},{32,48},{48,64},{64,80},{80,96},{96,112},{1... | collective-permute-start | bytes 786440 | tf_op jit(solution)/shard_map/ppermute | solution.py:374
  181.5 3.1 %collective-permute-done.28.refs_4_ = bf16[64,2048]{1,0:T(8,128)(2,1)S(1)} collective-permute-done((bf16[64,2048]{1,0:T(8,128)(2,1)S(1)}, bf16[64,2048]{1,0:T(8,128)(2,1)S(1)}, u32[]{:S(2)}, u32[]{:S(2)}) %collective-permute-start.28) | collective-permute-done | bytes 262176 | tf_op jit(solution)/shard_map/ppermute | solution.py:27
  186.4 7.4 %collective-permute-done.36 = bf16[64,2048]{1,0:T(8,128)(2,1)S(1)} collective-permute-done((bf16[64,2048]{1,0:T(8,128)(2,1)S(1)}, bf16[64,2048]{1,0:T(8,128)(2,1)S(1)}, u32[]{:S(2)}, u32[]{:S(2)}) %collective-permute-start.36) | collective-permute-done | bytes 262176 | tf_op jit(solution)/shard_map/ppermute | solution.py:374
  193.8 3.2 %collective-permute-done.29 = bf16[64,2048]{1,0:T(8,128)(2,1)S(1)} collective-permute-done((bf16[64,2048]{1,0:T(8,128)(2,1)S(1)}, bf16[64,2048]{1,0:T(8,128)(2,1)S(1)}, u32[]{:S(2)}, u32[]{:S(2)}) %collective-permute-start.29) | collective-permute-done | bytes 262176 | tf_op jit(solution)/shard_map/ppermute | solution.py:374
  (86 shorter events, 34.0 us)
Async XLA Ops:
  7.0 99.6 %collective-permute-start.13 = (bf16[3,448,2048]{2,1,0:T(8,128)(2,1)}, bf16[3,448,2048]{2,1,0:T(8,128)(2,1)}, u32[]{:S(2)}, u32[]{:S(2)}) collective-permute-start(bf16[3,448,2048]{2,1,0:T(8,128)(2,1)} %stack.42.refs_0_), channel_id=1, source_target_pairs={{0,1},{1,0},{2,3},{3,2},{4,5},{5,4},{6,7},{7,6},{8,9},{9,8},{10,11... | collective-permute-start | bytes 16515080 | tf_op jit(solution)/shard_map/ppermute | solution.py:43
  9.8 42.2 %all-to-all-start = ((bf16[16,128,384]{2,1,0:T(8,128)(2,1)}), bf16[16,128,384]{2,1,0:T(8,128)(2,1)S(1)}, u32[]{:S(2)}, u32[]{:S(2)}) async-start(bf16[16,128,384]{2,1,0:T(8,128)(2,1)} %pack.1), calls=%async_computation | async-start | bytes 3145728 | tf_op jit(solution)/shard_map/all_to_all | solution.py:336
  15.9 31.3 %collective-permute-start.1 = (bf16[128,2048]{1,0:T(8,128)(2,1)S(1)}, bf16[128,2048]{1,0:T(8,128)(2,1)}, u32[]{:S(2)}, u32[]{:S(2)}) collective-permute-start(bf16[128,2048]{1,0:T(8,128)(2,1)S(1)} %bitcast.30), channel_id=1, source_target_pairs={{0,6},{2,0},{4,2},{6,4},{8,14},{10,8},{12,10},{14,12},{1,7},{3,1},... | collective-permute-start | bytes 1572872 | tf_op jit(solution)/shard_map/ppermute | solution.py:27
  16.5 32.6 %collective-permute-start.2 = (bf16[128,2048]{1,0:T(8,128)(2,1)S(1)}, bf16[128,2048]{1,0:T(8,128)(2,1)}, u32[]{:S(2)}, u32[]{:S(2)}) collective-permute-start(bf16[128,2048]{1,0:T(8,128)(2,1)S(1)} %bitcast.31), channel_id=1, source_target_pairs={{0,8},{2,10},{4,12},{6,14},{8,0},{10,2},{12,4},{14,6},{1,9},{3,11}... | collective-permute-start | bytes 1572872 | tf_op jit(solution)/shard_map/ppermute | solution.py:27
  47.2 18.3 %collective-permute-start.4 = (bf16[128,2048]{1,0:T(8,128)(2,1)}, bf16[128,2048]{1,0:T(8,128)(2,1)S(1)}, u32[]{:S(2)}, u32[]{:S(2)}) collective-permute-start(bf16[128,2048]{1,0:T(8,128)(2,1)} %collective-permute-done.1.refs_2_), channel_id=1, source_target_pairs={{0,6},{2,0},{4,2},{6,4},{8,14},{10,8},{12,10},{14,12},{1,7},{3,1},... | collective-permute-start | bytes 1572872 | tf_op jit(solution)/shard_map/ppermute | solution.py:27
  47.6 20.0 %collective-permute-start.5 = (bf16[128,2048]{1,0:T(8,128)(2,1)}, bf16[128,2048]{1,0:T(8,128)(2,1)S(1)}, u32[]{:S(2)}, u32[]{:S(2)}) collective-permute-start(bf16[128,2048]{1,0:T(8,128)(2,1)} %collective-permute-done.1.refs_2_), channel_id=1, source_target_pairs={{0,8},{2,10},{4,12},{6,14},{8,0},{10,2},{12,4},{14,6},{1,9},{3,11}... | collective-permute-start | bytes 1572872 | tf_op jit(solution)/shard_map/ppermute | solution.py:27
  49.1 19.8 %collective-permute-start.3 = (bf16[128,2048]{1,0:T(8,128)(2,1)}, bf16[128,2048]{1,0:T(8,128)(2,1)S(1)}, u32[]{:S(2)}, u32[]{:S(2)}) collective-permute-start(bf16[128,2048]{1,0:T(8,128)(2,1)} %collective-permute-done.2.refs_3_), channel_id=1, source_target_pairs={{0,2},{2,4},{4,6},{6,0},{8,10},{10,12},{12,14},{14,8},{1,3},{3,5},... | collective-permute-start | bytes 1572872 | tf_op jit(solution)/shard_map/ppermute | solution.py:27
  50.5 26.9 %collective-permute-start = (bf16[128,2048]{1,0:T(8,128)(2,1)}, bf16[128,2048]{1,0:T(8,128)(2,1)}, u32[]{:S(2)}, u32[]{:S(2)}) collective-permute-start(bf16[128,2048]{1,0:T(8,128)(2,1)} %bitcast.29), channel_id=1, source_target_pairs={{0,2},{2,4},{4,6},{6,0},{8,10},{10,12},{12,14},{14,8},{1,3},{3,5},... | collective-permute-start | bytes 1572872 | tf_op jit(solution)/shard_map/ppermute | solution.py:27
  60.3 21.6 %all-to-all-start.1 = ((bf16[8,256,128]{2,1,0:T(8,128)(2,1)}), bf16[8,256,128]{2,1,0:T(8,128)(2,1)S(1)}, u32[]{:S(2)}, u32[]{:S(2)}) async-start(bf16[8,256,128]{2,1,0:T(8,128)(2,1)} %bitcast.33), calls=%async_computation.1 | async-start | bytes 1048576 | tf_op jit(solution)/shard_map/all_to_all | solution.py:343
  66.1 15.7 %collective-permute-start.6 = (bf16[48,2048]{1,0:T(8,128)(2,1)}, bf16[48,2048]{1,0:T(8,128)(2,1)S(1)}, u32[]{:S(2)}, u32[]{:S(2)}) collective-permute-start(bf16[48,2048]{1,0:T(8,128)(2,1)} %slice.24), channel_id=1, source_target_pairs={{0,8},{2,10},{4,12},{6,14},{8,0},{10,2},{12,4},{14,6},{1,9},{3,11}... | collective-permute-start | bytes 589832 | tf_op jit(solution)/shard_map/ppermute | solution.py:27
  68.3 13.6 %collective-permute-start.7 = (bf16[48,2048]{1,0:T(8,128)(2,1)}, bf16[48,2048]{1,0:T(8,128)(2,1)S(1)}, u32[]{:S(2)}, u32[]{:S(2)}) collective-permute-start(bf16[48,2048]{1,0:T(8,128)(2,1)} %slice.25), channel_id=1, source_target_pairs={{0,6},{2,0},{4,2},{6,4},{8,14},{10,8},{12,10},{14,12},{1,7},{3,1},... | collective-permute-start | bytes 589832 | tf_op jit(solution)/shard_map/ppermute | solution.py:27
  69.5 12.3 %collective-permute-start.8 = (bf16[32,2048]{1,0:T(8,128)(2,1)}, bf16[32,2048]{1,0:T(8,128)(2,1)}, u32[]{:S(2)}, u32[]{:S(2)}) collective-permute-start(bf16[32,2048]{1,0:T(8,128)(2,1)} %slice.26), channel_id=1, source_target_pairs={{0,2},{2,4},{4,6},{6,0},{8,10},{10,12},{12,14},{14,8},{1,3},{3,5},... | collective-permute-start | bytes 393224 | tf_op jit(solution)/shard_map/ppermute | solution.py:27
  88.9 14.0 %collective-permute-start.11 = (bf16[128,2048]{1,0:T(8,128)(2,1)S(1)}, bf16[128,2048]{1,0:T(8,128)(2,1)S(1)}, u32[]{:S(2)}, u32[]{:S(2)}) collective-permute-start(bf16[128,2048]{1,0:T(8,128)(2,1)S(1)} %get-tuple-element.49.refs_0_), channel_id=1, source_target_pairs={{0,6},{2,0},{4,2},{6,4},{8,14},{10,8},{12,10},{14,12},{1,7},{3,1},... | collective-permute-start | bytes 1572872 | tf_op jit(solution)/shard_map/ppermute | solution.py:27
  90.3 14.8 %collective-permute-start.12 = (bf16[128,2048]{1,0:T(8,128)(2,1)S(1)}, bf16[128,2048]{1,0:T(8,128)(2,1)S(1)}, u32[]{:S(2)}, u32[]{:S(2)}) collective-permute-start(bf16[128,2048]{1,0:T(8,128)(2,1)S(1)} %get-tuple-element.49.refs_0_), channel_id=1, source_target_pairs={{0,8},{2,10},{4,12},{6,14},{8,0},{10,2},{12,4},{14,6},{1,9},{3,11}... | collective-permute-start | bytes 1572872 | tf_op jit(solution)/shard_map/ppermute | solution.py:27
  90.9 19.8 %collective-permute-start.10 = (bf16[128,2048]{1,0:T(8,128)(2,1)S(1)}, bf16[128,2048]{1,0:T(8,128)(2,1)S(1)}, u32[]{:S(2)}, u32[]{:S(2)}) collective-permute-start(bf16[128,2048]{1,0:T(8,128)(2,1)S(1)} %get-tuple-element.49.refs_0_), channel_id=1, source_target_pairs={{0,2},{2,4},{4,6},{6,0},{8,10},{10,12},{12,14},{14,8},{1,3},{3,5},... | collective-permute-start | bytes 1572872 | tf_op jit(solution)/shard_map/ppermute | solution.py:27
  103.0 20.8 %collective-permute-start.14 = (bf16[128,2048]{1,0:T(8,128)(2,1)S(1)}, bf16[128,2048]{1,0:T(8,128)(2,1)S(1)}, u32[]{:S(2)}, u32[]{:S(2)}) collective-permute-start(bf16[128,2048]{1,0:T(8,128)(2,1)S(1)} %collective-permute-done.11.refs_2_), channel_id=1, source_target_pairs={{0,6},{2,0},{4,2},{6,4},{8,14},{10,8},{12,10},{14,12},{1,7},{3,1},... | collective-permute-start | bytes 1572872 | tf_op jit(solution)/shard_map/ppermute | solution.py:27
  104.3 19.5 %collective-permute-start.16 = (bf16[128,2048]{1,0:T(8,128)(2,1)S(1)}, bf16[128,2048]{1,0:T(8,128)(2,1)S(1)}, u32[]{:S(2)}, u32[]{:S(2)}) collective-permute-start(bf16[128,2048]{1,0:T(8,128)(2,1)S(1)} %collective-permute-done.11.refs_2_), channel_id=1, source_target_pairs={{0,8},{2,10},{4,12},{6,14},{8,0},{10,2},{12,4},{14,6},{1,9},{3,11}... | collective-permute-start | bytes 1572872 | tf_op jit(solution)/shard_map/ppermute | solution.py:27
  105.2 18.6 %collective-permute-start.15 = (bf16[128,2048]{1,0:T(8,128)(2,1)S(1)}, bf16[128,2048]{1,0:T(8,128)(2,1)S(1)}, u32[]{:S(2)}, u32[]{:S(2)}) collective-permute-start(bf16[128,2048]{1,0:T(8,128)(2,1)S(1)} %collective-permute-done.12.refs_3_), channel_id=1, source_target_pairs={{0,2},{2,4},{4,6},{6,0},{8,10},{10,12},{12,14},{14,8},{1,3},{3,5},... | collective-permute-start | bytes 1572872 | tf_op jit(solution)/shard_map/ppermute | solution.py:27
  135.3 9.8 %collective-permute-start.21 = (bf16[48,2048]{1,0:T(8,128)(2,1)S(1)}, bf16[48,2048]{1,0:T(8,128)(2,1)S(1)}, u32[]{:S(2)}, u32[]{:S(2)}) collective-permute-start(bf16[48,2048]{1,0:T(8,128)(2,1)S(1)} %get-tuple-element.73), channel_id=1, source_target_pairs={{0,8},{2,10},{4,12},{6,14},{8,0},{10,2},{12,4},{14,6},{1,9},{3,11}... | collective-permute-start | bytes 589832 | tf_op jit(solution)/shard_map/ppermute | solution.py:27
  136.3 8.8 %collective-permute-start.22 = (bf16[48,2048]{1,0:T(8,128)(2,1)S(1)}, bf16[48,2048]{1,0:T(8,128)(2,1)S(1)}, u32[]{:S(2)}, u32[]{:S(2)}) collective-permute-start(bf16[48,2048]{1,0:T(8,128)(2,1)S(1)} %get-tuple-element.74), channel_id=1, source_target_pairs={{0,2},{2,4},{4,6},{6,0},{8,10},{10,12},{12,14},{14,8},{1,3},{3,5},... | collective-permute-start | bytes 589832 | tf_op jit(solution)/shard_map/ppermute | solution.py:27
  145.3 9.7 %collective-permute-start.32 = (bf16[64,2048]{1,0:T(8,128)(2,1)S(1)}, bf16[64,2048]{1,0:T(8,128)(2,1)S(1)}, u32[]{:S(2)}, u32[]{:S(2)}) collective-permute-start(bf16[64,2048]{1,0:T(8,128)(2,1)S(1)} %get-tuple-element.84), channel_id=1, source_target_pairs={{0,8},{2,10},{4,12},{6,14},{8,0},{10,2},{12,4},{14,6},{1,9},{3,11}... | collective-permute-start | bytes 786440 | tf_op jit(solution)/shard_map/ppermute | solution.py:27
  146.5 9.6 %collective-permute-start.31 = (bf16[64,2048]{1,0:T(8,128)(2,1)S(1)}, bf16[64,2048]{1,0:T(8,128)(2,1)S(1)}, u32[]{:S(2)}, u32[]{:S(2)}) collective-permute-start(bf16[64,2048]{1,0:T(8,128)(2,1)S(1)} %get-tuple-element.83), channel_id=1, source_target_pairs={{0,2},{2,4},{4,6},{6,0},{8,10},{10,12},{12,14},{14,8},{1,3},{3,5},... | collective-permute-start | bytes 786440 | tf_op jit(solution)/shard_map/ppermute | solution.py:27
  149.7 28.0 %collective-permute-start.30 = (bf16[64,2048]{1,0:T(8,128)(2,1)S(1)}, bf16[64,2048]{1,0:T(8,128)(2,1)S(1)}, u32[]{:S(2)}, u32[]{:S(2)}) collective-permute-start(bf16[64,2048]{1,0:T(8,128)(2,1)S(1)} %get-tuple-element.81), channel_id=1, source_target_pairs={{0,6},{2,0},{4,2},{6,4},{8,14},{10,8},{12,10},{14,12},{1,7},{3,1},... | collective-permute-start | bytes 786440 | tf_op jit(solution)/shard_map/ppermute | solution.py:27
  149.7 31.5 %collective-permute-start.17 = (bf16[64,2048]{1,0:T(8,128)(2,1)S(1)}, bf16[64,2048]{1,0:T(8,128)(2,1)S(1)}, u32[]{:S(2)}, u32[]{:S(2)}) collective-permute-start(bf16[64,2048]{1,0:T(8,128)(2,1)S(1)} %get-tuple-element.59), channel_id=1, source_target_pairs={{0,6},{2,0},{4,2},{6,4},{8,14},{10,8},{12,10},{14,12},{1,7},{3,1},... | collective-permute-start | bytes 786440 | tf_op jit(solution)/shard_map/ppermute | solution.py:27
  151.8 15.4 %collective-permute-start.34 = (bf16[64,2048]{1,0:T(8,128)(2,1)S(1)}, bf16[64,2048]{1,0:T(8,128)(2,1)S(1)}, u32[]{:S(2)}, u32[]{:S(2)}) collective-permute-start(bf16[64,2048]{1,0:T(8,128)(2,1)S(1)} %get-tuple-element.86), channel_id=1, source_target_pairs={{0,6},{2,0},{4,2},{6,4},{8,14},{10,8},{12,10},{14,12},{1,7},{3,1},... | collective-permute-start | bytes 786440 | tf_op jit(solution)/shard_map/ppermute | solution.py:27
  155.0 12.2 %collective-permute-start.25 = (bf16[64,2048]{1,0:T(8,128)(2,1)S(1)}, bf16[64,2048]{1,0:T(8,128)(2,1)S(1)}, u32[]{:S(2)}, u32[]{:S(2)}) collective-permute-start(bf16[64,2048]{1,0:T(8,128)(2,1)S(1)} %get-tuple-element.77), channel_id=1, source_target_pairs={{0,8},{2,10},{4,12},{6,14},{8,0},{10,2},{12,4},{14,6},{1,9},{3,11}... | collective-permute-start | bytes 786440 | tf_op jit(solution)/shard_map/ppermute | solution.py:27
  156.1 14.1 %collective-permute-start.24 = (bf16[64,2048]{1,0:T(8,128)(2,1)S(1)}, bf16[64,2048]{1,0:T(8,128)(2,1)S(1)}, u32[]{:S(2)}, u32[]{:S(2)}) collective-permute-start(bf16[64,2048]{1,0:T(8,128)(2,1)S(1)} %get-tuple-element.76), channel_id=1, source_target_pairs={{0,2},{2,4},{4,6},{6,0},{8,10},{10,12},{12,14},{14,8},{1,3},{3,5},... | collective-permute-start | bytes 786440 | tf_op jit(solution)/shard_map/ppermute | solution.py:27
  167.1 7.3 %collective-permute-start.27 = (bf16[64,2048]{1,0:T(8,128)(2,1)S(1)}, bf16[64,2048]{1,0:T(8,128)(2,1)S(1)}, u32[]{:S(2)}, u32[]{:S(2)}) collective-permute-start(bf16[64,2048]{1,0:T(8,128)(2,1)S(1)} %get-tuple-element.79), channel_id=1, source_target_pairs={{0,6},{2,0},{4,2},{6,4},{8,14},{10,8},{12,10},{14,12},{1,7},{3,1},... | collective-permute-start | bytes 786440 | tf_op jit(solution)/shard_map/ppermute | solution.py:27
  167.2 11.5 %collective-permute-start.33 = (bf16[64,2048]{1,0:T(8,128)(2,1)S(1)}, bf16[64,2048]{1,0:T(8,128)(2,1)S(1)}, u32[]{:S(2)}, u32[]{:S(2)}) collective-permute-start(bf16[64,2048]{1,0:T(8,128)(2,1)S(1)} %add_convert_fusion.1), channel_id=1, source_target_pairs={{0,2},{2,4},{4,6},{6,0},{8,10},{10,12},{12,14},{14,8},{1,3},{3,5},... | collective-permute-start | bytes 786440 | tf_op jit(solution)/shard_map/ppermute | solution.py:27
  170.2 8.8 %collective-permute-start.35 = (bf16[64,2048]{1,0:T(8,128)(2,1)S(1)}, bf16[64,2048]{1,0:T(8,128)(2,1)S(1)}, u32[]{:S(2)}, u32[]{:S(2)}) collective-permute-start(bf16[64,2048]{1,0:T(8,128)(2,1)S(1)} %add_convert_fusion), channel_id=1, source_target_pairs={{0,8},{2,10},{4,12},{6,14},{8,0},{10,2},{12,4},{14,6},{1,9},{3,11}... | collective-permute-start | bytes 786440 | tf_op jit(solution)/shard_map/ppermute | solution.py:27
  179.3 14.5 %collective-permute-start.36 = (bf16[64,2048]{1,0:T(8,128)(2,1)S(1)}, bf16[64,2048]{1,0:T(8,128)(2,1)S(1)}, u32[]{:S(2)}, u32[]{:S(2)}) collective-permute-start(bf16[64,2048]{1,0:T(8,128)(2,1)S(1)} %finish.3), channel_id=1, source_target_pairs={{240,0},{0,16},{16,32},{32,48},{48,64},{64,80},{80,96},{96,112},{1... | collective-permute-start | bytes 786440 | tf_op jit(solution)/shard_map/ppermute | solution.py:374
  184.9 12.1 %collective-permute-start.29 = (bf16[64,2048]{1,0:T(8,128)(2,1)S(1)}, bf16[64,2048]{1,0:T(8,128)(2,1)S(1)}, u32[]{:S(2)}, u32[]{:S(2)}) collective-permute-start(bf16[64,2048]{1,0:T(8,128)(2,1)S(1)} %finish.2), channel_id=1, source_target_pairs={{240,0},{0,16},{16,32},{32,48},{48,64},{64,80},{80,96},{96,112},{1... | collective-permute-start | bytes 786440 | tf_op jit(solution)/shard_map/ppermute | solution.py:374
  (15 other events, 108.8 us)
where the time goes:
time: 198 us
  waiting for transfers between devices  83 us (42%)
  starting transfers between devices  61.7 us (31%)
  Pallas kernels  44.2 us (22%)
  local copies, waits for them, and re-layouts  7.49 us (4%)
    ppermute x33, waiting for transfers between devices, chip_shift(): return lax.ppermute(v, ('y', 'x'), route)  70.4 us
    ppermute x33, starting transfers between devices, chip_shift(): return lax.ppermute(v, ('y', 'x'), route)  46.9 us
    pallas_call x3, Pallas kernels, ffn(): pl.pallas_call(lambda *refs: ffn_kernel(n, *refs), out_shape=tuple((jax.S...  21.8 us
    ppermute x2, waiting for transfers between devices, layer(): lax.ppermute(total, 's', [((i - 1) % 16, i) for i in range(16)])  10.6 us
    pallas_call x1, Pallas kernels, attend(): pl.pallas_call(attend_kernel, out_shape=jax.ShapeDtypeStruct((2048, HEAD_...  7.47 us
    pallas_call x2, Pallas kernels, stack(): pl.pallas_call(lambda *refs: stack_kernel(axis, *refs), out_shape=jax.Sha...  6.67 us
    all_to_all x1, starting transfers between devices, layer(): qkv = lax.all_to_all(packed, SEQ, split_axis=0, concat_axis=0, tiled=True)  6.07 us
    unnamed x16, local copies, waits for them, and re-layouts  5.3 us
  transfers between devices with their start and end apart: 39, of which 15 were waited for; matrix products, arithmetic and copies ran while one was open for 1% of the time, Pallas kernels for 19%

commit v1 on v0

--- a/solution.py
+++ b/solution.py
@@ -90,7 +90,7 @@
 
 
 def attend_kernel(qkv, out):
-    scale = HEAD_DIM ** -0.5
+    rate = HEAD_DIM ** -0.5 * 1.4426950408889634
     row = lax.broadcasted_iota(jnp.int32, (QB, SPAN), 0)
     col = lax.broadcasted_iota(jnp.int32, (QB, SPAN), 1)
     dims = (((1,), (1,)), ((), ()))
@@ -100,17 +100,17 @@
         def block(j, carry, lo=lo, hi=hi):
             rows = pl.ds(lo + j * QB, QB)
             q = qkv[rows, 0:128]
-            sd = lax.dot_general(q, qkv[lo:hi, 128:256], dims, preferred_element_type=F32) * scale
+            sd = lax.dot_general(q, qkv[lo:hi, 128:256], dims, preferred_element_type=F32)
             sd = jnp.where(col <= row + j * QB, sd, -1e30)
             top = jnp.max(sd, axis=-1, keepdims=True)
             if lo > 0:
-                sl = lax.dot_general(q, qkv[0:lo, 128:256], dims, preferred_element_type=F32) * scale
+                sl = lax.dot_general(q, qkv[0:lo, 128:256], dims, preferred_element_type=F32)
                 top = jnp.maximum(top, jnp.max(sl, axis=-1, keepdims=True))
-            ed = jnp.exp(sd - top)
+            ed = jnp.exp2((sd - top) * rate)
             total = jnp.sum(ed, axis=-1, keepdims=True)
             mix = jnp.dot(ed.astype(BF), qkv[lo:hi, 256:384], preferred_element_type=F32)
             if lo > 0:
-                el = jnp.exp(sl - top)
+                el = jnp.exp2((sl - top) * rate)
                 total = total + jnp.sum(el, axis=-1, keepdims=True)
                 mix = mix + jnp.dot(el.astype(BF), qkv[0:lo, 256:384], preferred_element_type=F32)
             out[rows, :] = (mix / total).astype(BF)
@@ -238,7 +238,7 @@
         x[row : row + v.shape[0], :] = v[...]
         row += v.shape[0]
 
-    block = min(x.shape[0], 128) if x.shape[0] == 512 else x.shape[0]
+    block = min(x.shape[0], 256) if x.shape[0] == 512 else x.shape[0]
 
     def step(i, carry):
         part = i % 2
@@ -349,6 +349,7 @@
     residual, normed = norm(mine, to_core(theirs), stream[0], norm_gain)
 
     first = gather_first(normed)
+    first[0, 1], first[1, 0], weights = lax.optimization_barrier((first[0, 1], first[1, 0], weights))
     second = gather_second(first)
     outs = ffn([first[k] for k in FIRST], weights, [H] * (4 * SPLIT))
     outs, second = lax.optimization_barrier((outs, second))

time: 198 us -> 196 us (0.990)
  the two profiles are of different devices: /device:TPU:4 before, /device:TPU:30 now
where the time goes in v1:
time: 196 us
  waiting for transfers between devices  96.1 us (49%)
  starting transfers between devices  52 us (27%)
  Pallas kernels  38.9 us (20%)
  local copies, waits for them, and re-layouts  7.49 us (4%)
    ppermute x33, waiting for transfers between devices, chip_shift(): return lax.ppermute(v, ('y', 'x'), route)  84.2 us
    ppermute x33, starting transfers between devices, chip_shift(): return lax.ppermute(v, ('y', 'x'), route)  38.7 us
    pallas_call x3, Pallas kernels, ffn(): pl.pallas_call(lambda *refs: ffn_kernel(n, *refs), out_shape=tuple((jax.S...  16.7 us
    ppermute x2, waiting for transfers between devices, layer(): lax.ppermute(total, 's', [((i - 1) % 16, i) for i in range(16)])  9.96 us
    pallas_call x1, Pallas kernels, attend(): pl.pallas_call(attend_kernel, out_shape=jax.ShapeDtypeStruct((2048, HEAD_...  7.29 us
    pallas_call x2, Pallas kernels, stack(): pl.pallas_call(lambda *refs: stack_kernel(axis, *refs), out_shape=jax.Sha...  6.67 us
    all_to_all x1, starting transfers between devices, layer(): lax.all_to_all(blocks, ('y', 'x'), split_axis=0, concat_axis=0, tiled=True)  6.14 us
    all_to_all x1, starting transfers between devices, layer(): qkv = lax.all_to_all(packed, SEQ, split_axis=0, concat_axis=0, tiled=True)  5.93 us
  transfers between devices with their start and end apart: 39, of which 17 were waited for; matrix products, arithmetic and copies ran while one was open for 1% of the time, Pallas kernels for 17%

profile of v1, /device:TPU:30, one launch (start us, length us, event | category | flops | bytes accessed | tf_op | source)
XLA Modules:
  0.0 195.9 jit_solution(14570769357384531092)
XLA Ops:
  4.5 2.5 %stack.42.refs_0_ = bf16[3,448,2048]{2,1,0:T(8,128)(2,1)} custom-call(bf16[448,2048]{1,0:T(8,128)(2,1)S(1)} %bitcast.25, bf16[448,2048]{1,0:T(8,128)(2,1)S(1)} %bitcast.26, bf16[448,2048]{1,0:T(8,128)(2,1)S(1)} %bitcast.27), custom_call_target="tpu_custom_call" | custom-call | tf_op jit(solution)/shard_map/stack/pallas_call | solution.py:219
  7.1 2.7 %pack.1 = bf16[16,128,384]{2,1,0:T(8,128)(2,1)} custom-call(bf16[128,2048]{1,0:T(8,128)(2,1)} %bitcast.35, bf16[128,2048]{1,0:T(8,128)(2,1)} %bitcast.36, bf16[128,2048]{1,0:T(8,128)(2,1)} %bitcast.37), custom_call_target="tpu_custom_call" | custom-call | tf_op jit(solution)/shard_map/pack/pallas_call | solution.py:78
  9.8 5.9 %all-to-all-start = ((bf16[16,128,384]{2,1,0:T(8,128)(2,1)}), bf16[16,128,384]{2,1,0:T(8,128)(2,1)S(1)}, u32[]{:S(2)}, u32[]{:S(2)}) async-start(bf16[16,128,384]{2,1,0:T(8,128)(2,1)} %pack.1), calls=%async_computation | async-start | bytes 3145728 | tf_op jit(solution)/shard_map/all_to_all | solution.py:336
  17.2 28.8 %collective-permute-done.1.refs_2_ = bf16[128,2048]{1,0:T(8,128)(2,1)} collective-permute-done((bf16[128,2048]{1,0:T(8,128)(2,1)S(1)}, bf16[128,2048]{1,0:T(8,128)(2,1)}, u32[]{:S(2)}, u32[]{:S(2)}) %collective-permute-start.1) | collective-permute-done | bytes 524320 | tf_op jit(solution)/shard_map/ppermute | solution.py:27
  46.0 1.7 collective-permute-start.4
  50.9 7.3 %attend.1 = bf16[2048,128]{1,0:T(8,128)(2,1)S(1)} custom-call(bf16[2048,384]{1,0:T(8,128)(2,1)S(1)} %bitcast.28), custom_call_target="tpu_custom_call" | custom-call | flops 1200000000 | bytes 2097152 | tf_op jit(solution)/shard_map/attend/pallas_call | solution.py:123
  59.0 6.1 %all-to-all-start.1 = ((bf16[8,256,128]{2,1,0:T(8,128)(2,1)}), bf16[8,256,128]{2,1,0:T(8,128)(2,1)S(1)}, u32[]{:S(2)}, u32[]{:S(2)}) async-start(bf16[8,256,128]{2,1,0:T(8,128)(2,1)} %bitcast.33), calls=%async_computation.1 | async-start | bytes 1048576 | tf_op jit(solution)/shard_map/all_to_all | solution.py:343
  68.6 2.4 %collective-permute-start.8 = (bf16[32,2048]{1,0:T(8,128)(2,1)}, bf16[32,2048]{1,0:T(8,128)(2,1)}, u32[]{:S(2)}, u32[]{:S(2)}) collective-permute-start(bf16[32,2048]{1,0:T(8,128)(2,1)} %slice.26), channel_id=1, source_target_pairs={{0,2},{2,4},{4,6},{6,0},{8,10},{10,12},{12,14},{14,8},{1,3},{3,5},... | collective-permute-start | bytes 393224 | tf_op jit(solution)/shard_map/ppermute | solution.py:27
  71.1 5.2 %collective-permute-done.refs_1_ = bf16[128,2048]{1,0:T(8,128)(2,1)} collective-permute-done((bf16[128,2048]{1,0:T(8,128)(2,1)}, bf16[128,2048]{1,0:T(8,128)(2,1)}, u32[]{:S(2)}, u32[]{:S(2)}) %collective-permute-start) | collective-permute-done | bytes 524320 | tf_op jit(solution)/shard_map/ppermute | solution.py:27
  76.3 5.0 %collective-permute-done.8.refs_9_ = bf16[32,2048]{1,0:T(8,128)(2,1)} collective-permute-done((bf16[32,2048]{1,0:T(8,128)(2,1)}, bf16[32,2048]{1,0:T(8,128)(2,1)}, u32[]{:S(2)}, u32[]{:S(2)}) %collective-permute-start.8) | collective-permute-done | bytes 131104 | tf_op jit(solution)/shard_map/ppermute | solution.py:27
  81.3 4.6 %project.1 = (f32[128,2048]{1,0:T(8,128)S(1)}, bf16[128,2048]{1,0:T(8,128)(2,1)S(1)}) custom-call(s32[9]{0:T(128)S(1)} %stack.41.place, bf16[8,256,128]{2,1,0:T(8,128)(2,1)S(1)} %all-to-all-done.1.att, bf16[128,2048]{1,0:T(8,128)(2,1)S(1)} %bitcast.32, bf16[128,2048]{1,0:T(8,128)(2,1)} %collective-permute-done.refs_1_, ...), custom_call_target="tpu_custom_call" | custom-call | flops 1100000000 | bytes 6000000 | tf_op jit(solution)/shard_map/project/pallas_call | solution.py:169
  86.0 1.9 collective-permute-done.9.other
  90.3 2.7 %collective-permute-start.10 = (bf16[128,2048]{1,0:T(8,128)(2,1)S(1)}, bf16[128,2048]{1,0:T(8,128)(2,1)S(1)}, u32[]{:S(2)}, u32[]{:S(2)}) collective-permute-start(bf16[128,2048]{1,0:T(8,128)(2,1)S(1)} %get-tuple-element.52.refs_0_), channel_id=1, source_target_pairs={{0,2},{2,4},{4,6},{6,0},{8,10},{10,12},{12,14},{14,8},{1,3},{3,5},... | collective-permute-start | bytes 1572872 | tf_op jit(solution)/shard_map/ppermute | solution.py:27
  93.0 4.2 %stack.43.refs_4_.refs_3_ = bf16[3,2,448,2048]{3,2,1,0:T(8,128)(2,1)S(1)} custom-call(bf16[3,448,2048]{2,1,0:T(8,128)(2,1)} %stack.42.refs_0_, bf16[3,448,2048]{2,1,0:T(8,128)(2,1)} %collective-permute-done.13.refs_1_), custom_call_target="tpu_custom_call" | custom-call | tf_op jit(solution)/shard_map/stack/pallas_call | solution.py:219
  97.2 6.6 %collective-permute-done.11.refs_2_ = bf16[128,2048]{1,0:T(8,128)(2,1)S(1)} collective-permute-done((bf16[128,2048]{1,0:T(8,128)(2,1)S(1)}, bf16[128,2048]{1,0:T(8,128)(2,1)S(1)}, u32[]{:S(2)}, u32[]{:S(2)}) %collective-permute-start.11) | collective-permute-done | bytes 524320 | tf_op jit(solution)/shard_map/ppermute | solution.py:27
  105.3 2.8 %collective-permute-start.15 = (bf16[128,2048]{1,0:T(8,128)(2,1)S(1)}, bf16[128,2048]{1,0:T(8,128)(2,1)S(1)}, u32[]{:S(2)}, u32[]{:S(2)}) collective-permute-start(bf16[128,2048]{1,0:T(8,128)(2,1)S(1)} %collective-permute-done.12.refs_3_), channel_id=1, source_target_pairs={{0,2},{2,4},{4,6},{6,0},{8,10},{10,12},{12,14},{14,8},{1,3},{3,5},... | collective-permute-start | bytes 1572872 | tf_op jit(solution)/shard_map/ppermute | solution.py:27
  108.2 7.9 %ffn.3 = (bf16[64,2048]{1,0:T(8,128)(2,1)S(1)}, bf16[64,2048]{1,0:T(8,128)(2,1)S(1)}, bf16[64,2048]{1,0:T(8,128)(2,1)S(1)}, bf16[64,2048]{1,0:T(8,128)(2,1)S(1)}...) custom-call(bf16[128,2048]{1,0:T(8,128)(2,1)S(1)} %get-tuple-element, ...), custom_call_target="tpu_custom_call" | custom-call | flops 5637144576 | bytes 4194304 | tf_op jit(solution)/shard_map/ffn/pallas_call | solution.py:265
  116.1 2.2 %collective-permute-done.14.refs_1_ = bf16[128,2048]{1,0:T(8,128)(2,1)S(1)} collective-permute-done((bf16[128,2048]{1,0:T(8,128)(2,1)S(1)}, bf16[128,2048]{1,0:T(8,128)(2,1)S(1)}, u32[]{:S(2)}, u32[]{:S(2)}) %collective-permute-start.14) | collective-permute-done | bytes 524320 | tf_op jit(solution)/shard_map/ppermute | solution.py:27
  121.2 2.1 %collective-permute-start.20 = (bf16[32,2048]{1,0:T(8,128)(2,1)S(1)}, bf16[32,2048]{1,0:T(8,128)(2,1)S(1)}, u32[]{:S(2)}, u32[]{:S(2)}) collective-permute-start(bf16[32,2048]{1,0:T(8,128)(2,1)S(1)} %slice.23), channel_id=1, source_target_pairs={{0,2},{2,4},{4,6},{6,0},{8,10},{10,12},{12,14},{14,8},{1,3},{3,5},... | collective-permute-start | bytes 393224 | tf_op jit(solution)/shard_map/ppermute | solution.py:27
  123.3 2.9 %collective-permute-done.20.refs_2_ = bf16[32,2048]{1,0:T(8,128)(2,1)S(1)} collective-permute-done((bf16[32,2048]{1,0:T(8,128)(2,1)S(1)}, bf16[32,2048]{1,0:T(8,128)(2,1)S(1)}, u32[]{:S(2)}, u32[]{:S(2)}) %collective-permute-start.20) | collective-permute-done | bytes 131104 | tf_op jit(solution)/shard_map/ppermute | solution.py:27
  126.8 3.2 %ffn.4 = (bf16[48,2048]{1,0:T(8,128)(2,1)S(1)}, bf16[48,2048]{1,0:T(8,128)(2,1)S(1)}, bf16[32,2048]{1,0:T(8,128)(2,1)S(1)}) custom-call(bf16[48,2048]{1,0:T(8,128)(2,1)S(1)} %collective-permute-done.18.refs_0_, bf16[48,2048]{1,0:T(8,128)(2,1)S(1)} %collective-permute-done.19.refs_1_, bf16[32,2048]{1,0:T(8,128)(2,1)S(1)} %collective-permute-done.20.refs_2_, ...), custom_call_target="tpu_custom_call" | custom-call | flops 1409286144 | bytes 1048576 | tf_op jit(solution)/shard_map/ffn/pallas_call | solution.py:265
  131.1 2.6 %collective-permute-start.22 = (bf16[48,2048]{1,0:T(8,128)(2,1)S(1)}, bf16[48,2048]{1,0:T(8,128)(2,1)S(1)}, u32[]{:S(2)}, u32[]{:S(2)}) collective-permute-start(bf16[48,2048]{1,0:T(8,128)(2,1)S(1)} %get-tuple-element.80), channel_id=1, source_target_pairs={{0,2},{2,4},{4,6},{6,0},{8,10},{10,12},{12,14},{14,8},{1,3},{3,5},... | collective-permute-start | bytes 589832 | tf_op jit(solution)/shard_map/ppermute | solution.py:27
  133.8 5.5 %ffn.5 = (bf16[128,2048]{1,0:T(8,128)(2,1)S(1)}, bf16[128,2048]{1,0:T(8,128)(2,1)S(1)}, bf16[128,2048]{1,0:T(8,128)(2,1)S(1)}) custom-call(bf16[128,2048]{1,0:T(8,128)(2,1)S(1)} %collective-permute-done.15.refs_0_, bf16[128,2048]{1,0:T(8,128)(2,1)S(1)} %collective-permute-done.14.refs_1_, bf16[128,2048]{1,0:T(8,128)(2,1)S(1)} %collective-permute-done.16.refs_2_, ...), custom_call_target="tpu_custom_call" | custom-call | flops 4227858432 | bytes 3145728 | tf_op jit(solution)/shard_map/ffn/pallas_call | solution.py:265
  140.1 2.7 %collective-permute-start.24 = (bf16[64,2048]{1,0:T(8,128)(2,1)S(1)}, bf16[64,2048]{1,0:T(8,128)(2,1)S(1)}, u32[]{:S(2)}, u32[]{:S(2)}) collective-permute-start(bf16[64,2048]{1,0:T(8,128)(2,1)S(1)} %get-tuple-element.82), channel_id=1, source_target_pairs={{0,2},{2,4},{4,6},{6,0},{8,10},{10,12},{12,14},{14,8},{1,3},{3,5},... | collective-permute-start | bytes 786440 | tf_op jit(solution)/shard_map/ppermute | solution.py:27
  145.4 3.0 %collective-permute-done.24 = bf16[64,2048]{1,0:T(8,128)(2,1)S(1)} collective-permute-done((bf16[64,2048]{1,0:T(8,128)(2,1)S(1)}, bf16[64,2048]{1,0:T(8,128)(2,1)S(1)}, u32[]{:S(2)}, u32[]{:S(2)}) %collective-permute-start.24) | collective-permute-done | bytes 262176 | tf_op jit(solution)/shard_map/ppermute | solution.py:27
  149.2 2.9 %collective-permute-start.31 = (bf16[64,2048]{1,0:T(8,128)(2,1)S(1)}, bf16[64,2048]{1,0:T(8,128)(2,1)S(1)}, u32[]{:S(2)}, u32[]{:S(2)}) collective-permute-start(bf16[64,2048]{1,0:T(8,128)(2,1)S(1)} %get-tuple-element.89), channel_id=1, source_target_pairs={{0,2},{2,4},{4,6},{6,0},{8,10},{10,12},{12,14},{14,8},{1,3},{3,5},... | collective-permute-start | bytes 786440 | tf_op jit(solution)/shard_map/ppermute | solution.py:27
  152.2 10.4 %collective-permute-done.27 = bf16[64,2048]{1,0:T(8,128)(2,1)S(1)} collective-permute-done((bf16[64,2048]{1,0:T(8,128)(2,1)S(1)}, bf16[64,2048]{1,0:T(8,128)(2,1)S(1)}, u32[]{:S(2)}, u32[]{:S(2)}) %collective-permute-start.27) | collective-permute-done | bytes 262176 | tf_op jit(solution)/shard_map/ppermute | solution.py:27
  163.5 1.9 collective-permute-done.34
  166.4 4.4 %collective-permute-done.32 = bf16[64,2048]{1,0:T(8,128)(2,1)S(1)} collective-permute-done((bf16[64,2048]{1,0:T(8,128)(2,1)S(1)}, bf16[64,2048]{1,0:T(8,128)(2,1)S(1)}, u32[]{:S(2)}, u32[]{:S(2)}) %collective-permute-start.32) | collective-permute-done | bytes 262176 | tf_op jit(solution)/shard_map/ppermute | solution.py:27
  171.7 3.0 %collective-permute-done.28.refs_4_ = bf16[64,2048]{1,0:T(8,128)(2,1)S(1)} collective-permute-done((bf16[64,2048]{1,0:T(8,128)(2,1)S(1)}, bf16[64,2048]{1,0:T(8,128)(2,1)S(1)}, u32[]{:S(2)}, u32[]{:S(2)}) %collective-permute-start.28) | collective-permute-done | bytes 262176 | tf_op jit(solution)/shard_map/ppermute | solution.py:27
  175.8 9.0 %collective-permute-done.35.refs_4_ = bf16[64,2048]{1,0:T(8,128)(2,1)S(1)} collective-permute-done((bf16[64,2048]{1,0:T(8,128)(2,1)S(1)}, bf16[64,2048]{1,0:T(8,128)(2,1)S(1)}, u32[]{:S(2)}, u32[]{:S(2)}) %collective-permute-start.35) | collective-permute-done | bytes 262176 | tf_op jit(solution)/shard_map/ppermute | solution.py:27
  185.1 10.0 %collective-permute-done.36 = bf16[64,2048]{1,0:T(8,128)(2,1)S(1)} collective-permute-done((bf16[64,2048]{1,0:T(8,128)(2,1)S(1)}, bf16[64,2048]{1,0:T(8,128)(2,1)S(1)}, u32[]{:S(2)}, u32[]{:S(2)}) %collective-permute-start.36) | collective-permute-done | bytes 262176 | tf_op jit(solution)/shard_map/ppermute | solution.py:375
  (86 shorter events, 31.4 us)
Async XLA Ops:
  7.0 86.0 %collective-permute-start.13 = (bf16[3,448,2048]{2,1,0:T(8,128)(2,1)}, bf16[3,448,2048]{2,1,0:T(8,128)(2,1)}, u32[]{:S(2)}, u32[]{:S(2)}) collective-permute-start(bf16[3,448,2048]{2,1,0:T(8,128)(2,1)} %stack.42.refs_0_), channel_id=1, source_target_pairs={{0,1},{1,0},{2,3},{3,2},{4,5},{5,4},{6,7},{7,6},{8,9},{9,8},{10,11... | collective-permute-start | bytes 16515080 | tf_op jit(solution)/shard_map/ppermute | solution.py:43
  9.8 41.1 %all-to-all-start = ((bf16[16,128,384]{2,1,0:T(8,128)(2,1)}), bf16[16,128,384]{2,1,0:T(8,128)(2,1)S(1)}, u32[]{:S(2)}, u32[]{:S(2)}) async-start(bf16[16,128,384]{2,1,0:T(8,128)(2,1)} %pack.1), calls=%async_computation | async-start | bytes 3145728 | tf_op jit(solution)/shard_map/all_to_all | solution.py:336
  15.8 30.3 %collective-permute-start.1 = (bf16[128,2048]{1,0:T(8,128)(2,1)S(1)}, bf16[128,2048]{1,0:T(8,128)(2,1)}, u32[]{:S(2)}, u32[]{:S(2)}) collective-permute-start(bf16[128,2048]{1,0:T(8,128)(2,1)S(1)} %bitcast.30), channel_id=1, source_target_pairs={{0,6},{2,0},{4,2},{6,4},{8,14},{10,8},{12,10},{14,12},{1,7},{3,1},... | collective-permute-start | bytes 1572872 | tf_op jit(solution)/shard_map/ppermute | solution.py:27
  16.7 31.8 %collective-permute-start.2 = (bf16[128,2048]{1,0:T(8,128)(2,1)S(1)}, bf16[128,2048]{1,0:T(8,128)(2,1)}, u32[]{:S(2)}, u32[]{:S(2)}) collective-permute-start(bf16[128,2048]{1,0:T(8,128)(2,1)S(1)} %bitcast.31), channel_id=1, source_target_pairs={{0,8},{2,10},{4,12},{6,14},{8,0},{10,2},{12,4},{14,6},{1,9},{3,11}... | collective-permute-start | bytes 1572872 | tf_op jit(solution)/shard_map/ppermute | solution.py:27
  46.0 19.1 %collective-permute-start.4 = (bf16[128,2048]{1,0:T(8,128)(2,1)}, bf16[128,2048]{1,0:T(8,128)(2,1)S(1)}, u32[]{:S(2)}, u32[]{:S(2)}) collective-permute-start(bf16[128,2048]{1,0:T(8,128)(2,1)} %collective-permute-done.1.refs_2_), channel_id=1, source_target_pairs={{0,6},{2,0},{4,2},{6,4},{8,14},{10,8},{12,10},{14,12},{1,7},{3,1},... | collective-permute-start | bytes 1572872 | tf_op jit(solution)/shard_map/ppermute | solution.py:27
  47.8 18.6 %collective-permute-start.5 = (bf16[128,2048]{1,0:T(8,128)(2,1)}, bf16[128,2048]{1,0:T(8,128)(2,1)S(1)}, u32[]{:S(2)}, u32[]{:S(2)}) collective-permute-start(bf16[128,2048]{1,0:T(8,128)(2,1)} %collective-permute-done.1.refs_2_), channel_id=1, source_target_pairs={{0,8},{2,10},{4,12},{6,14},{8,0},{10,2},{12,4},{14,6},{1,9},{3,11}... | collective-permute-start | bytes 1572872 | tf_op jit(solution)/shard_map/ppermute | solution.py:27
  48.5 19.5 %collective-permute-start.3 = (bf16[128,2048]{1,0:T(8,128)(2,1)}, bf16[128,2048]{1,0:T(8,128)(2,1)S(1)}, u32[]{:S(2)}, u32[]{:S(2)}) collective-permute-start(bf16[128,2048]{1,0:T(8,128)(2,1)} %collective-permute-done.2.refs_3_), channel_id=1, source_target_pairs={{0,2},{2,4},{4,6},{6,0},{8,10},{10,12},{12,14},{14,8},{1,3},{3,5},... | collective-permute-start | bytes 1572872 | tf_op jit(solution)/shard_map/ppermute | solution.py:27
  50.0 26.3 %collective-permute-start = (bf16[128,2048]{1,0:T(8,128)(2,1)}, bf16[128,2048]{1,0:T(8,128)(2,1)}, u32[]{:S(2)}, u32[]{:S(2)}) collective-permute-start(bf16[128,2048]{1,0:T(8,128)(2,1)} %bitcast.29), channel_id=1, source_target_pairs={{0,2},{2,4},{4,6},{6,0},{8,10},{10,12},{12,14},{14,8},{1,3},{3,5},... | collective-permute-start | bytes 1572872 | tf_op jit(solution)/shard_map/ppermute | solution.py:27
  59.0 22.3 %all-to-all-start.1 = ((bf16[8,256,128]{2,1,0:T(8,128)(2,1)}), bf16[8,256,128]{2,1,0:T(8,128)(2,1)S(1)}, u32[]{:S(2)}, u32[]{:S(2)}) async-start(bf16[8,256,128]{2,1,0:T(8,128)(2,1)} %bitcast.33), calls=%async_computation.1 | async-start | bytes 1048576 | tf_op jit(solution)/shard_map/all_to_all | solution.py:343
  65.8 15.4 %collective-permute-start.6 = (bf16[48,2048]{1,0:T(8,128)(2,1)}, bf16[48,2048]{1,0:T(8,128)(2,1)S(1)}, u32[]{:S(2)}, u32[]{:S(2)}) collective-permute-start(bf16[48,2048]{1,0:T(8,128)(2,1)} %slice.24), channel_id=1, source_target_pairs={{0,8},{2,10},{4,12},{6,14},{8,0},{10,2},{12,4},{14,6},{1,9},{3,11}... | collective-permute-start | bytes 589832 | tf_op jit(solution)/shard_map/ppermute | solution.py:27
  67.1 14.2 %collective-permute-start.7 = (bf16[48,2048]{1,0:T(8,128)(2,1)}, bf16[48,2048]{1,0:T(8,128)(2,1)S(1)}, u32[]{:S(2)}, u32[]{:S(2)}) collective-permute-start(bf16[48,2048]{1,0:T(8,128)(2,1)} %slice.25), channel_id=1, source_target_pairs={{0,6},{2,0},{4,2},{6,4},{8,14},{10,8},{12,10},{14,12},{1,7},{3,1},... | collective-permute-start | bytes 589832 | tf_op jit(solution)/shard_map/ppermute | solution.py:27
  68.6 12.6 %collective-permute-start.8 = (bf16[32,2048]{1,0:T(8,128)(2,1)}, bf16[32,2048]{1,0:T(8,128)(2,1)}, u32[]{:S(2)}, u32[]{:S(2)}) collective-permute-start(bf16[32,2048]{1,0:T(8,128)(2,1)} %slice.26), channel_id=1, source_target_pairs={{0,2},{2,4},{4,6},{6,0},{8,10},{10,12},{12,14},{14,8},{1,3},{3,5},... | collective-permute-start | bytes 393224 | tf_op jit(solution)/shard_map/ppermute | solution.py:27
  88.3 15.4 %collective-permute-start.11 = (bf16[128,2048]{1,0:T(8,128)(2,1)S(1)}, bf16[128,2048]{1,0:T(8,128)(2,1)S(1)}, u32[]{:S(2)}, u32[]{:S(2)}) collective-permute-start(bf16[128,2048]{1,0:T(8,128)(2,1)S(1)} %get-tuple-element.52.refs_0_), channel_id=1, source_target_pairs={{0,6},{2,0},{4,2},{6,4},{8,14},{10,8},{12,10},{14,12},{1,7},{3,1},... | collective-permute-start | bytes 1572872 | tf_op jit(solution)/shard_map/ppermute | solution.py:27
  88.9 14.9 %collective-permute-start.12 = (bf16[128,2048]{1,0:T(8,128)(2,1)S(1)}, bf16[128,2048]{1,0:T(8,128)(2,1)S(1)}, u32[]{:S(2)}, u32[]{:S(2)}) collective-permute-start(bf16[128,2048]{1,0:T(8,128)(2,1)S(1)} %get-tuple-element.52.refs_0_), channel_id=1, source_target_pairs={{0,8},{2,10},{4,12},{6,14},{8,0},{10,2},{12,4},{14,6},{1,9},{3,11}... | collective-permute-start | bytes 1572872 | tf_op jit(solution)/shard_map/ppermute | solution.py:27
  90.3 17.9 %collective-permute-start.10 = (bf16[128,2048]{1,0:T(8,128)(2,1)S(1)}, bf16[128,2048]{1,0:T(8,128)(2,1)S(1)}, u32[]{:S(2)}, u32[]{:S(2)}) collective-permute-start(bf16[128,2048]{1,0:T(8,128)(2,1)S(1)} %get-tuple-element.52.refs_0_), channel_id=1, source_target_pairs={{0,2},{2,4},{4,6},{6,0},{8,10},{10,12},{12,14},{14,8},{1,3},{3,5},... | collective-permute-start | bytes 1572872 | tf_op jit(solution)/shard_map/ppermute | solution.py:27
  103.8 14.5 %collective-permute-start.14 = (bf16[128,2048]{1,0:T(8,128)(2,1)S(1)}, bf16[128,2048]{1,0:T(8,128)(2,1)S(1)}, u32[]{:S(2)}, u32[]{:S(2)}) collective-permute-start(bf16[128,2048]{1,0:T(8,128)(2,1)S(1)} %collective-permute-done.11.refs_2_), channel_id=1, source_target_pairs={{0,6},{2,0},{4,2},{6,4},{8,14},{10,8},{12,10},{14,12},{1,7},{3,1},... | collective-permute-start | bytes 1572872 | tf_op jit(solution)/shard_map/ppermute | solution.py:27
  103.9 14.4 %collective-permute-start.16 = (bf16[128,2048]{1,0:T(8,128)(2,1)S(1)}, bf16[128,2048]{1,0:T(8,128)(2,1)S(1)}, u32[]{:S(2)}, u32[]{:S(2)}) collective-permute-start(bf16[128,2048]{1,0:T(8,128)(2,1)S(1)} %collective-permute-done.11.refs_2_), channel_id=1, source_target_pairs={{0,8},{2,10},{4,12},{6,14},{8,0},{10,2},{12,4},{14,6},{1,9},{3,11}... | collective-permute-start | bytes 1572872 | tf_op jit(solution)/shard_map/ppermute | solution.py:27
  105.3 13.0 %collective-permute-start.15 = (bf16[128,2048]{1,0:T(8,128)(2,1)S(1)}, bf16[128,2048]{1,0:T(8,128)(2,1)S(1)}, u32[]{:S(2)}, u32[]{:S(2)}) collective-permute-start(bf16[128,2048]{1,0:T(8,128)(2,1)S(1)} %collective-permute-done.12.refs_3_), channel_id=1, source_target_pairs={{0,2},{2,4},{4,6},{6,0},{8,10},{10,12},{12,14},{14,8},{1,3},{3,5},... | collective-permute-start | bytes 1572872 | tf_op jit(solution)/shard_map/ppermute | solution.py:27
  130.1 9.9 %collective-permute-start.21 = (bf16[48,2048]{1,0:T(8,128)(2,1)S(1)}, bf16[48,2048]{1,0:T(8,128)(2,1)S(1)}, u32[]{:S(2)}, u32[]{:S(2)}) collective-permute-start(bf16[48,2048]{1,0:T(8,128)(2,1)S(1)} %get-tuple-element.79), channel_id=1, source_target_pairs={{0,8},{2,10},{4,12},{6,14},{8,0},{10,2},{12,4},{14,6},{1,9},{3,11}... | collective-permute-start | bytes 589832 | tf_op jit(solution)/shard_map/ppermute | solution.py:27
  131.1 8.8 %collective-permute-start.22 = (bf16[48,2048]{1,0:T(8,128)(2,1)S(1)}, bf16[48,2048]{1,0:T(8,128)(2,1)S(1)}, u32[]{:S(2)}, u32[]{:S(2)}) collective-permute-start(bf16[48,2048]{1,0:T(8,128)(2,1)S(1)} %get-tuple-element.80), channel_id=1, source_target_pairs={{0,2},{2,4},{4,6},{6,0},{8,10},{10,12},{12,14},{14,8},{1,3},{3,5},... | collective-permute-start | bytes 589832 | tf_op jit(solution)/shard_map/ppermute | solution.py:27
  140.1 8.3 %collective-permute-start.24 = (bf16[64,2048]{1,0:T(8,128)(2,1)S(1)}, bf16[64,2048]{1,0:T(8,128)(2,1)S(1)}, u32[]{:S(2)}, u32[]{:S(2)}) collective-permute-start(bf16[64,2048]{1,0:T(8,128)(2,1)S(1)} %get-tuple-element.82), channel_id=1, source_target_pairs={{0,2},{2,4},{4,6},{6,0},{8,10},{10,12},{12,14},{14,8},{1,3},{3,5},... | collective-permute-start | bytes 786440 | tf_op jit(solution)/shard_map/ppermute | solution.py:27
  143.9 27.7 %collective-permute-start.17 = (bf16[64,2048]{1,0:T(8,128)(2,1)S(1)}, bf16[64,2048]{1,0:T(8,128)(2,1)S(1)}, u32[]{:S(2)}, u32[]{:S(2)}) collective-permute-start(bf16[64,2048]{1,0:T(8,128)(2,1)S(1)} %get-tuple-element.65), channel_id=1, source_target_pairs={{0,6},{2,0},{4,2},{6,4},{8,14},{10,8},{12,10},{14,12},{1,7},{3,1},... | collective-permute-start | bytes 786440 | tf_op jit(solution)/shard_map/ppermute | solution.py:27
  143.9 31.9 %collective-permute-start.30 = (bf16[64,2048]{1,0:T(8,128)(2,1)S(1)}, bf16[64,2048]{1,0:T(8,128)(2,1)S(1)}, u32[]{:S(2)}, u32[]{:S(2)}) collective-permute-start(bf16[64,2048]{1,0:T(8,128)(2,1)S(1)} %get-tuple-element.87), channel_id=1, source_target_pairs={{0,6},{2,0},{4,2},{6,4},{8,14},{10,8},{12,10},{14,12},{1,7},{3,1},... | collective-permute-start | bytes 786440 | tf_op jit(solution)/shard_map/ppermute | solution.py:27
  143.9 18.7 %collective-permute-start.27 = (bf16[64,2048]{1,0:T(8,128)(2,1)S(1)}, bf16[64,2048]{1,0:T(8,128)(2,1)S(1)}, u32[]{:S(2)}, u32[]{:S(2)}) collective-permute-start(bf16[64,2048]{1,0:T(8,128)(2,1)S(1)} %get-tuple-element.85), channel_id=1, source_target_pairs={{0,6},{2,0},{4,2},{6,4},{8,14},{10,8},{12,10},{14,12},{1,7},{3,1},... | collective-permute-start | bytes 786440 | tf_op jit(solution)/shard_map/ppermute | solution.py:27
  148.4 17.0 %collective-permute-start.34 = (bf16[64,2048]{1,0:T(8,128)(2,1)S(1)}, bf16[64,2048]{1,0:T(8,128)(2,1)S(1)}, u32[]{:S(2)}, u32[]{:S(2)}) collective-permute-start(bf16[64,2048]{1,0:T(8,128)(2,1)S(1)} %get-tuple-element.92), channel_id=1, source_target_pairs={{0,6},{2,0},{4,2},{6,4},{8,14},{10,8},{12,10},{14,12},{1,7},{3,1},... | collective-permute-start | bytes 786440 | tf_op jit(solution)/shard_map/ppermute | solution.py:27
  149.2 17.1 %collective-permute-start.31 = (bf16[64,2048]{1,0:T(8,128)(2,1)S(1)}, bf16[64,2048]{1,0:T(8,128)(2,1)S(1)}, u32[]{:S(2)}, u32[]{:S(2)}) collective-permute-start(bf16[64,2048]{1,0:T(8,128)(2,1)S(1)} %get-tuple-element.89), channel_id=1, source_target_pairs={{0,2},{2,4},{4,6},{6,0},{8,10},{10,12},{12,14},{14,8},{1,3},{3,5},... | collective-permute-start | bytes 786440 | tf_op jit(solution)/shard_map/ppermute | solution.py:27
  165.4 9.2 %collective-permute-start.28 = (bf16[64,2048]{1,0:T(8,128)(2,1)S(1)}, bf16[64,2048]{1,0:T(8,128)(2,1)S(1)}, u32[]{:S(2)}, u32[]{:S(2)}) collective-permute-start(bf16[64,2048]{1,0:T(8,128)(2,1)S(1)} %add_convert_fusion.2), channel_id=1, source_target_pairs={{0,8},{2,10},{4,12},{6,14},{8,0},{10,2},{12,4},{14,6},{1,9},{3,11}... | collective-permute-start | bytes 786440 | tf_op jit(solution)/shard_map/ppermute | solution.py:27
  166.3 8.3 %collective-permute-start.26 = (bf16[64,2048]{1,0:T(8,128)(2,1)S(1)}, bf16[64,2048]{1,0:T(8,128)(2,1)S(1)}, u32[]{:S(2)}, u32[]{:S(2)}) collective-permute-start(bf16[64,2048]{1,0:T(8,128)(2,1)S(1)} %add_convert_fusion.3), channel_id=1, source_target_pairs={{0,2},{2,4},{4,6},{6,0},{8,10},{10,12},{12,14},{14,8},{1,3},{3,5},... | collective-permute-start | bytes 786440 | tf_op jit(solution)/shard_map/ppermute | solution.py:27
  170.8 14.0 %collective-permute-start.35 = (bf16[64,2048]{1,0:T(8,128)(2,1)S(1)}, bf16[64,2048]{1,0:T(8,128)(2,1)S(1)}, u32[]{:S(2)}, u32[]{:S(2)}) collective-permute-start(bf16[64,2048]{1,0:T(8,128)(2,1)S(1)} %add_convert_fusion), channel_id=1, source_target_pairs={{0,8},{2,10},{4,12},{6,14},{8,0},{10,2},{12,4},{14,6},{1,9},{3,11}... | collective-permute-start | bytes 786440 | tf_op jit(solution)/shard_map/ppermute | solution.py:27
  171.6 13.2 %collective-permute-start.33 = (bf16[64,2048]{1,0:T(8,128)(2,1)S(1)}, bf16[64,2048]{1,0:T(8,128)(2,1)S(1)}, u32[]{:S(2)}, u32[]{:S(2)}) collective-permute-start(bf16[64,2048]{1,0:T(8,128)(2,1)S(1)} %add_convert_fusion.1), channel_id=1, source_target_pairs={{0,2},{2,4},{4,6},{6,0},{8,10},{10,12},{12,14},{14,8},{1,3},{3,5},... | collective-permute-start | bytes 786440 | tf_op jit(solution)/shard_map/ppermute | solution.py:27
  174.8 10.3 %collective-permute-start.29 = (bf16[64,2048]{1,0:T(8,128)(2,1)S(1)}, bf16[64,2048]{1,0:T(8,128)(2,1)S(1)}, u32[]{:S(2)}, u32[]{:S(2)}) collective-permute-start(bf16[64,2048]{1,0:T(8,128)(2,1)S(1)} %finish.2), channel_id=1, source_target_pairs={{240,0},{0,16},{16,32},{32,48},{48,64},{64,80},{80,96},{96,112},{1... | collective-permute-start | bytes 786440 | tf_op jit(solution)/shard_map/ppermute | solution.py:375
  185.0 10.1 %collective-permute-start.36 = (bf16[64,2048]{1,0:T(8,128)(2,1)S(1)}, bf16[64,2048]{1,0:T(8,128)(2,1)S(1)}, u32[]{:S(2)}, u32[]{:S(2)}) collective-permute-start(bf16[64,2048]{1,0:T(8,128)(2,1)S(1)} %finish.3), channel_id=1, source_target_pairs={{240,0},{0,16},{16,32},{32,48},{48,64},{64,80},{80,96},{96,112},{1... | collective-permute-start | bytes 786440 | tf_op jit(solution)/shard_map/ppermute | solution.py:375
  (15 other events, 110.3 us)
